TPU v7x, 768 devices: a whole 4x8x12 slice. The times are simulated.
768 devices in a mesh: rows: 96 (over y, z), cols: 8 (over x, core).
Axes of the slice: x: 4, y: 8, z: 12, core: 2. Of those that a mesh axis runs over, the one named last changes fastest.
Arguments:
- users: bfloat16 [196608, 256], P('rows'), may hold values from -0.3984375 to 0.3984375
- items: bfloat16 [8, 1536, 256], P('cols'), may hold values from -6 to 6
- ratings: bfloat16 [96, 8, 64, 128, 128], P('rows', 'cols'), may hold values from -6 to 6
- tile_users: int32 [96, 8, 64], P('rows', 'cols'), may hold values from 0 to 15
- tile_items: int32 [96, 8, 64], P('rows', 'cols'), may hold values from 0 to 11
- tile_count: int32 [96, 8], P('rows', 'cols'), may hold values from 16 to 64, as said below
- send_list: int32 [96, 8, 8, 1], P('rows', 'cols'), may hold values from 0 to 11
- block_target: int32 [96, 8, 8], P('rows', 'cols'), may hold values from 0 to 11
- similarity: bfloat16 [96, 8, 8, 128, 128], P('rows', 'cols'), may hold values from -6 to 6
Outputs:
- new_items: float32 [8, 1536, 256], P('cols', 'rows')
Inputs may be any that keep to these rules, and one draw needn't show every extreme that they name: `tile_count`: every draw has some device with all 64 slots live; the device differs from draw to draw.
All inputs are finite; a program needn't handle non-finite values.
Results may differ from a plain program's by a relative error of at most 0.00065.
Values may be sent and summed in bfloat16 or wider, within the bound.
A program may use at most 32 MiB of HBM per device.

v0:
```python
import jax
import jax.numpy as jnp
from jax import lax
from jax.sharding import PartitionSpec as P


def shards(
    users, items, ratings, tile_users, tile_items, tile_count, send_list, block_target, similarity
):
    rank = items.shape[2]
    icount = items.shape[1]
    tile = ratings.shape[-1]
    panels = items[0].reshape(-1, tile, rank)
    ntiles = panels.shape[0]
    user_tiles = users.reshape(-1, tile, rank)
    tiles_here = ratings.shape[2]
    width = min(16, tiles_here)
    nblocks = tiles_here // width
    live_count = tile_count[0, 0]
    tile_ids = jnp.arange(ntiles, dtype=jnp.int32)
    outgoing = panels[send_list[0, 0]]
    incoming = lax.all_to_all(outgoing, "cols", split_axis=0, concat_axis=0, tiled=True)
    blocks = similarity.shape[2]
    incoming = incoming.reshape(blocks, tile, rank)
    contrib = jnp.einsum(
        "kab,kbr->kar", similarity[0, 0], incoming, preferred_element_type=jnp.float32
    )
    targets = (tile_ids[:, None] == block_target[0, 0][None, :]).astype(jnp.float32)
    start_grad = jnp.einsum("kt,tbr->kbr", targets, contrib, precision=lax.Precision.HIGHEST)

    def tile_block(grad, pieces):
        user_idx, item_idx, rating, places = pieces
        left = user_tiles[user_idx]
        right = panels[item_idx]
        pred = jnp.einsum("tar,tbr->tab", left, right, preferred_element_type=jnp.float32)
        live = (places < live_count).astype(jnp.float32)
        err = ((pred - rating.astype(jnp.float32)) * live[:, None, None]).astype(jnp.bfloat16)
        part = jnp.einsum("tab,tar->tbr", err, left, preferred_element_type=jnp.float32)
        onehot = (tile_ids[:, None] == item_idx[None, :]).astype(jnp.float32)
        grad = grad + jnp.einsum("kt,tbr->kbr", onehot, part, precision=lax.Precision.HIGHEST)
        return (grad, None)

    inputs = (
        tile_users[0, 0].reshape(nblocks, width),
        tile_items[0, 0].reshape(nblocks, width),
        ratings[0, 0].reshape(nblocks, width, tile, tile),
        jnp.arange(tiles_here, dtype=jnp.int32).reshape(nblocks, width),
    )
    grad, unused = lax.scan(tile_block, start_grad, inputs)
    flat = grad.reshape(icount, rank)
    item_dev = icount // lax.axis_size("rows")
    total_entries = lax.axis_size("cols") * icount * rank
    owned = lax.psum_scatter(flat, "rows", scatter_dimension=0, tiled=True)
    squares = lax.psum(jnp.sum(owned * owned), ("rows", "cols"))
    meansq = squares / total_entries
    mine = lax.dynamic_slice_in_dim(
        items[0], lax.axis_index("rows") * item_dev, item_dev, 0
    ).astype(jnp.float32)
    updated = mine - 0.5 * owned / jnp.sqrt(meansq + 1e-06)
    return updated[None]


def solution(mesh):
    in_specs = (
        P("rows", None),
        P("cols", None, None),
        P("rows", "cols", None, None, None),
        P("rows", "cols", None),
        P("rows", "cols", None),
        P("rows", "cols"),
        P("rows", "cols", None, None),
        P("rows", "cols", None),
        P("rows", "cols", None, None, None),
    )
    out_specs = P("cols", "rows", None)
    return jax.shard_map(shards, mesh=mesh, in_specs=in_specs, out_specs=out_specs, check_vma=False)
```

profile of v0, /device:TPU:1, one launch (start us, length us, event | category | flops | bytes accessed | tf_op | source)
XLA Modules:
  0.0 873.3 jit_solution(12558821942346140669)
XLA Ops:
  6.5 0.7 fusion.32
  7.3 2.5 gather_fusion.2
  9.8 13.9 %all-to-all-start = ((bf16[8,1,128,256]{3,2,1,0:T(8,128)(2,1)}), bf16[8,1,128,256]{3,2,1,0:T(8,128)(2,1)S(1)}, u32[]{:S(2)}, u32[]{:S(2)}) async-start(bf16[8,1,128,256]{3,2,1,0:T(8,128)(2,1)} %bitcast.6), calls=%async_computation | async-start | bytes 1048576 | tf_op jit(solution)/shard_map/all_to_all | solution.py:22
  24.3 0.7 reduce.6
  25.1 0.7 reduce.7
  25.9 7.3 all-to-all-done
  34.0 2.4 fusion.23
  36.5 50.4 %while.11 = (s32[]{:T(128)}, f32[12,128,256]{2,0,1:T(8,128)}, s32[4,16]{1,0:T(4,128)S(1)}, s32[4,16]{1,0:T(4,128)S(1)}, bf16[16,128,256]{2,1,0:T(8,128)(2,1)}, /...) while((s32[]{:T(128)}, f32[12,128,256]{2,0,1:T(8,128)}, ...), condition=%wide.region_1.2_spmd.clone, body=%wide.region_0.1_spmd.clone.sunk | while | flops 345377088 | bytes 15214517 | solution.py:49
  36.5 1.8 gather_fusion
  38.3 2.7 gather_fusion.1
  41.1 0.7 fusion.52
  41.7 2.1 fusion.53
  43.8 5.2 fusion.55
  49.1 1.8 gather_fusion
  50.9 2.7 gather_fusion.1
  53.7 0.7 fusion.52
  54.3 2.1 fusion.53
  56.4 5.2 fusion.55
  61.7 1.8 gather_fusion
  63.5 2.7 gather_fusion.1
  66.3 0.7 fusion.52
  66.9 2.1 fusion.53
  69.0 5.2 fusion.55
  74.3 1.8 gather_fusion
  76.1 2.7 gather_fusion.1
  79.5 2.1 fusion.53
  81.6 5.2 fusion.55
  86.9 3.7 copy.11
  90.6 663.7 %reduce-scatter.2.cloned.1.call-done = f32[16,256]{1,0:T(8,128)} async-done(((f32[1536,256]{1,0:T(8,128)}), f32[16,256]{1,0:T(8,128)}) %reduce-scatter.2.cloned.1.call-update) | async-done | bytes 16400 | tf_op jit(solution)/shard_map/reduce_scatter | solution.py:53
  754.2 1.3 multiply_reduce_fusion
  755.5 108.9 %psum.7 = f32[]{:T(128)} all-reduce(f32[]{:T(128)} %multiply_reduce_fusion), channel_id=1, replica_groups=mesh['rows'=96,'cols'=8] {'rows','cols'}, use_global_device_ids=true, to_apply=%region_4.5 | all-reduce | flops 1 | bytes 8 | tf_op jit(solution)/shard_map/psum | solution.py:54
  865.1 1.3 fusion.28
  (34 shorter events, 2.4 us)
Async XLA Ops:
  6.5 26.6 %copy-start = (bf16[1,1,8,128,128]{4,3,2,1,0:T(8,128)(2,1)S(1)}, bf16[1,1,8,128,128]{4,3,2,1,0:T(8,128)(2,1)}, u32[]{:S(2)}) copy-start(bf16[1,1,8,128,128]{4,3,2,1,0:T(8,128)(2,1)} %param.19) | copy-start | bytes 786436
  6.5 17.7 %copy-start.2 = (s32[1,1,64]{2,1,0:T(1,128)S(1)}, s32[1,1,64]{2,1,0:T(1,128)}, u32[]{:S(2)}) copy-start(s32[1,1,64]{2,1,0:T(1,128)} %param.15) | copy-start | bytes 772
  6.5 18.5 %copy-start.3 = (s32[1,1,64]{2,1,0:T(1,128)S(1)}, s32[1,1,64]{2,1,0:T(1,128)}, u32[]{:S(2)}) copy-start(s32[1,1,64]{2,1,0:T(1,128)} %param.14) | copy-start | bytes 772
  9.8 23.4 %all-to-all-start = ((bf16[8,1,128,256]{3,2,1,0:T(8,128)(2,1)}), bf16[8,1,128,256]{3,2,1,0:T(8,128)(2,1)S(1)}, u32[]{:S(2)}, u32[]{:S(2)}) async-start(bf16[8,1,128,256]{3,2,1,0:T(8,128)(2,1)} %bitcast.6), calls=%async_computation | async-start | bytes 1048576 | tf_op jit(solution)/shard_map/all_to_all | solution.py:22
  23.7 10.3 %copy-start.1 = (s32[1,1,8]{2,1,0:T(1,128)S(1)}, s32[1,1,8]{2,1,0:T(1,128)}, u32[]{:S(2)}) copy-start(s32[1,1,8]{2,1,0:T(1,128)} %param.18) | copy-start | bytes 100
  23.7 730.6 %reduce-scatter.2.cloned.1.call-start = ((), (), s32[]{:S(2)}) async-start(), calls=%async_computation.2 | async-start | bytes 1589248 | tf_op jit(solution)/shard_map/reduce_scatter | solution.py:53
Sparse Core Ops, SparseCore 0:
  90.7 663.4 reduce-scatter.1
where the time goes:
time: 874 us; the launch traced here: 873 us
  waiting for transfers between devices  671 us (77%)
  blocking collectives  109 us (12%)
  matrix products  32 us (4%)
  local copies, waits for them, and re-layouts  25.7 us (3%)
  between operations  14.1 us (2%)
  starting transfers between devices  13.9 us (2%)
    reduce_scatter x1, waiting for transfers between devices, shards(): owned = lax.psum_scatter(flat, 'rows', scatter_dimension=0, tiled=True)  664 us
    psum x1, blocking collectives, shards(): squares = lax.psum(jnp.sum(owned * owned), ('rows', 'cols'))  109 us
    dot_general x4, matrix products, tile_block(): jnp.einsum('kt,tbr->kbr', onehot, part, precision=lax.Precision.HIGHEST)  20.9 us
  transfers between devices with their start and end apart: 2, of which 2 were waited for; matrix products, arithmetic and copies ran while one was open for 0% of the time, Pallas kernels for 0%

commit v1 on v0

v1 whole, which is shorter than its diff:
```python
import functools

import jax
import jax.numpy as jnp
from jax import lax
from jax.experimental import pallas as pl
from jax.experimental.pallas import tpu as pltpu
from jax.sharding import PartitionSpec as P

NZ = 12
UNROLL = 4
MESH = pl.DeviceIdType.MESH
VMEM = pltpu.VMEM
F32 = jnp.float32
BF16 = jnp.bfloat16


def tiles_kernel(tu, ti, cnt, users, items, ratings, grad):
    grad[...] = jnp.zeros_like(grad)
    count = cnt[0]

    def step(g, carry):
        for u in range(UNROLL):
            t = g * UNROLL + u
            i = ti[t]
            left = users[tu[t]]
            pred = lax.dot_general(
                left, items[i], (((1,), (1,)), ((), ())), preferred_element_type=F32
            )
            err = jnp.where(t < count, pred - ratings[t].astype(F32), 0.0).astype(BF16)
            part = lax.dot_general(
                err, left, (((0,), (0,)), ((), ())), preferred_element_type=F32
            )
            grad[i] += part
        return carry

    lax.fori_loop(0, (count + UNROLL - 1) // UNROLL, step, 0)


def graph_kernel(blocks, target, similarity, incoming, grad_in, grad):
    grad[...] = grad_in[...]
    for k in range(blocks):
        grad[target[k]] += jnp.dot(
            similarity[k], incoming[k], preferred_element_type=F32
        )


def reduce_kernel(
    ny, nz, nc, grad, items, out,
    send_a, send_b, recv_a, recv_b, acc_a, acc_b, recv2_a, recv2_b,
    sq, recv_z, recv_y, recv_c, mine,
    ssem, rsem, lsem,
):
    row = lax.axis_index("rows")
    col = lax.axis_index("cols")
    y = row // nz
    z = lax.rem(row, nz)
    half = acc_a.shape[-1]

    load = pltpu.make_async_copy(items.at[row], mine, lsem)
    load.start()

    def along_z(d):
        other = lax.rem(z + d, nz)
        return other, {"rows": y * nz + other}

    def along_y(d):
        other = lax.rem(y + d, ny)
        return other, {"rows": other * nz + z}

    def along_c(d):
        other = lax.rem(col + d, nc)
        return other, {"cols": other}

    barrier = pltpu.get_barrier_semaphore()
    for size, along in ((nz, along_z), (ny, along_y), (nc, along_c)):
        for d in range(1, size):
            pl.semaphore_signal(barrier, inc=1, device_id=along(d)[1], device_id_type=MESH)
    pl.semaphore_wait(barrier, nz + ny + nc - 3)

    def push(src, dst, which, device):
        copy = pltpu.make_async_remote_copy(
            src_ref=src, dst_ref=dst, send_sem=ssem.at[which], recv_sem=rsem.at[which],
            device_id=device, device_id_type=MESH,
        )
        copy.start()

    def whole(src, dst, which):
        return pltpu.make_async_remote_copy(
            src_ref=src, dst_ref=dst, send_sem=ssem.at[which], recv_sem=rsem.at[which],
            device_id={"cols": lax.rem(col + 1, nc)}, device_id_type=MESH,
        )

    for d in range(1, max(ny, nz)):
        if d < nz:
            other, device = along_z(d)
            send_a[d - 1] = grad[:, other, :, :half].astype(BF16)
            push(send_a.at[d - 1], recv_a.at[d - 1], 0, device)
        if d < ny:
            other, device = along_y(d)
            send_b[d - 1] = grad[other, :, :, half:]
            push(send_b.at[d - 1], recv_b.at[d - 1], 1, device)

    whole(send_b, recv_b, 1).wait_recv()
    total = grad[y, :, :, half:]
    for d in range(ny - 1):
        total = total + recv_b[d]
    acc_b[...] = total
    for d in range(1, nz):
        other, device = along_z(d)
        push(acc_b.at[other], recv2_b.at[d - 1], 2, device)

    whole(send_a, recv_a, 0).wait_recv()
    total = grad[:, z, :, :half]
    for d in range(nz - 1):
        total = total + recv_a[d].astype(F32)
    acc_a[...] = total
    for d in range(1, ny):
        other, device = along_y(d)
        push(acc_a.at[other], recv2_a.at[d - 1], 3, device)

    whole(acc_b.at[pl.ds(0, nz - 1)], recv2_b, 2).wait_recv()
    own_b = acc_b[z]
    for d in range(nz - 1):
        own_b = own_b + recv2_b[d]
    whole(acc_a.at[pl.ds(0, ny - 1)], recv2_a, 3).wait_recv()
    own_a = acc_a[y]
    for d in range(ny - 1):
        own_a = own_a + recv2_a[d]

    part = jnp.sum(own_a * own_a + own_b * own_b, axis=0, keepdims=True)
    for n, (size, along, recv) in enumerate(
        ((nz, along_z, recv_z), (ny, along_y, recv_y), (nc, along_c, recv_c))
    ):
        sq[n] = part
        for d in range(1, size):
            push(sq.at[n], recv.at[d - 1], 4 + n, along(d)[1])
        whole(recv, recv, 4 + n).wait_recv()
        for d in range(size - 1):
            part = part + recv[d]
    entries = nc * ny * nz * out.shape[0] * out.shape[1]
    meansq = jnp.sum(part, axis=1, keepdims=True) / entries
    root = jnp.sqrt(meansq + 1e-06)

    load.wait()
    mixed = mine[...].astype(F32)
    out[:, :half] = mixed[:, :half] - 0.5 * own_a / root
    out[:, half:] = mixed[:, half:] - 0.5 * own_b / root

    whole(send_a, recv_a, 0).wait_send()
    whole(send_b, recv_b, 1).wait_send()
    whole(acc_b.at[pl.ds(0, nz - 1)], recv2_b, 2).wait_send()
    whole(acc_a.at[pl.ds(0, ny - 1)], recv2_a, 3).wait_send()
    for n, recv in enumerate((recv_z, recv_y, recv_c)):
        whole(recv, recv, 4 + n).wait_send()


def shards(
    users, items, ratings, tile_users, tile_items, tile_count, send_list, block_target, similarity
):
    icount, rank = items.shape[1:]
    tile = ratings.shape[-1]
    slots = ratings.shape[2]
    blocks = similarity.shape[2]
    ntiles = icount // tile
    nrows = lax.axis_size("rows")
    ncols = lax.axis_size("cols")
    nz = NZ
    ny = nrows // nz
    chunk = icount // nrows
    half = rank // 2
    panels = items[0].reshape(ntiles, tile, rank)
    smem = pl.BlockSpec(memory_space=pltpu.SMEM)
    vmem = pl.BlockSpec(memory_space=VMEM)
    grad_shape = jax.ShapeDtypeStruct((ntiles, tile, rank), F32)

    outgoing = panels[send_list[0, 0].reshape(-1)]
    incoming = lax.all_to_all(outgoing, "cols", split_axis=0, concat_axis=0, tiled=True)

    grad = pl.pallas_call(
        tiles_kernel,
        out_shape=grad_shape,
        in_specs=[smem, smem, smem, vmem, vmem, vmem],
        out_specs=vmem,
        compiler_params=pltpu.CompilerParams(vmem_limit_bytes=32 << 20),
        cost_estimate=pl.CostEstimate(
            flops=4 * slots * tile * tile * rank,
            bytes_accessed=2 * (users.size + items.size + ratings.size) + 4 * icount * rank,
            transcendentals=0,
        ),
        name="rating_tiles",
    )(
        tile_users[0, 0], tile_items[0, 0], tile_count[0],
        users.reshape(-1, tile, rank), panels, ratings[0, 0],
    )
    grad = pl.pallas_call(
        functools.partial(graph_kernel, blocks),
        out_shape=grad_shape,
        in_specs=[smem, vmem, vmem, vmem],
        out_specs=vmem,
        compiler_params=pltpu.CompilerParams(vmem_limit_bytes=32 << 20),
        name="graph_blocks",
    )(block_target[0, 0], similarity[0, 0], incoming.reshape(blocks, tile, rank), grad)

    updated = pl.pallas_call(
        functools.partial(reduce_kernel, ny, nz, ncols),
        out_shape=jax.ShapeDtypeStruct((chunk, rank), F32),
        in_specs=[vmem, pl.BlockSpec(memory_space=pl.ANY)],
        out_specs=vmem,
        scratch_shapes=[
            VMEM((nz - 1, ny, chunk, half), BF16),
            VMEM((ny - 1, nz, chunk, half), F32),
            VMEM((nz - 1, ny, chunk, half), BF16),
            VMEM((ny - 1, nz, chunk, half), F32),
            VMEM((ny, chunk, half), F32),
            VMEM((nz, chunk, half), F32),
            VMEM((ny - 1, chunk, half), F32),
            VMEM((nz - 1, chunk, half), F32),
            VMEM((3, 1, half), F32),
            VMEM((nz - 1, 1, half), F32),
            VMEM((ny - 1, 1, half), F32),
            VMEM((ncols - 1, 1, half), F32),
            VMEM((chunk, rank), BF16),
            pltpu.SemaphoreType.DMA((7,)),
            pltpu.SemaphoreType.DMA((7,)),
            pltpu.SemaphoreType.DMA,
        ],
        compiler_params=pltpu.CompilerParams(
            collective_id=0, has_side_effects=True, vmem_limit_bytes=32 << 20
        ),
        name="reduce_update",
    )(grad.reshape(ny, nz, chunk, rank), items[0].reshape(nrows, chunk, rank))
    return updated[None]


def solution(mesh):
    in_specs = (
        P("rows", None),
        P("cols", None, None),
        P("rows", "cols", None, None, None),
        P("rows", "cols", None),
        P("rows", "cols", None),
        P("rows", "cols"),
        P("rows", "cols", None, None),
        P("rows", "cols", None),
        P("rows", "cols", None, None, None),
    )
    out_specs = P("cols", "rows", None)
    return jax.shard_map(shards, mesh=mesh, in_specs=in_specs, out_specs=out_specs, check_vma=False)
```

time: 874 us -> 82.8 us (0.09)
  waiting for transfers between devices: 671 us -> 0.01 us
  blocking collectives: 109 us -> 0 us
  Pallas kernels: 0 us -> 61.2 us
  matrix products: 32 us -> 0 us
  local copies, waits for them, and re-layouts: 25.7 us -> 5.95 us
  between operations: 14.1 us -> 0.74 us
    reduce_scatter x1 -> x0, waiting for transfers between devices: 664 us -> none  [shards(): owned = lax.psum_scatter(flat, 'rows', scatter_dimension=0, tiled=True)]
    psum x1 -> x0, blocking collectives: 109 us -> none  [shards(): squares = lax.psum(jnp.sum(owned * owned), ('rows', 'cols'))]
    pallas_call x0 -> x3, Pallas kernels: none -> 61.2 us  [the longest x1 53.1 us: shards(): pl.pallas_call(functools.partial(reduce_kernel, ny, nz, ncols), out_shape...]
    dot_general x10 -> x0, matrix products: 32 us -> none  [the longest x4 20.9 us: tile_block(): jnp.einsum('kt,tbr->kbr', onehot, part, precision=lax.Precision.HIGHEST)]
    gather x9 -> x1, local copies, waits for them, and re-layouts: 20.8 us -> 2.51 us  [shards(): outgoing = panels[send_list[0, 0].reshape(-1)]]
  transfers between devices with their start and end apart: 2 -> 1, of which waited for: 2 -> 0; matrix products, arithmetic and copies ran while one was open for 0% -> 0% of each run, Pallas kernels for 0% -> 9%
where the time goes in v1:
time: 82.8 us; the launch traced here: 82.5 us
  Pallas kernels  61.2 us (74%)
  starting transfers between devices  13.9 us (17%)
  local copies, waits for them, and re-layouts  5.95 us (7%)
    pallas_call x1, Pallas kernels, shards(): pl.pallas_call(functools.partial(reduce_kernel, ny, nz, ncols), out_shape...  53.1 us
    all_to_all x1, starting transfers between devices, shards(): lax.all_to_all(outgoing, 'cols', split_axis=0, concat_axis=0, tiled=True)  13.9 us
    pallas_call x1, Pallas kernels, shards(): pl.pallas_call(tiles_kernel, out_shape=grad_shape, in_specs=[smem, smem,...  7.23 us
    unnamed x15, local copies, waits for them, and re-layouts  3.44 us
    gather x1, local copies, waits for them, and re-layouts, shards(): outgoing = panels[send_list[0, 0].reshape(-1)]  2.51 us
  transfers between devices with their start and end apart: 1, of which 0 were waited for; matrix products, arithmetic and copies ran while one was open for 0% of the time, Pallas kernels for 9%

profile of v1, /device:TPU:1, one launch (start us, length us, event | category | flops | bytes accessed | tf_op | source)
XLA Modules:
  0.0 82.5 jit_solution(10590925056041238105)
XLA Ops:
  0.0 0.0 copy-start
  0.0 0.0 copy-start.5
  0.0 0.0 copy-start.4
  0.0 0.7 fusion
  0.7 2.5 %gather_fusion = bf16[8,128,256]{2,1,0:T(8,128)(2,1)} fusion(bf16[12,128,256]{2,1,0:T(8,128)(2,1)} %bitcast.17, s32[1024]{0:T(1024)S(1)} %pad_clamp_fusion), kind=kCustom, calls=%fused_computation | custom fusion | bytes 1048608 | tf_op jit(solution)/shard_map/gather | solution.py:177
  3.3 13.9 %all-to-all-start = ((bf16[8,128,256]{2,1,0:T(8,128)(2,1)}), bf16[8,128,256]{2,1,0:T(8,128)(2,1)S(1)}, u32[]{:S(2)}, u32[]{:S(2)}) async-start(bf16[8,128,256]{2,1,0:T(8,128)(2,1)} %gather_fusion), calls=%async_computation | async-start | bytes 1048576 | tf_op jit(solution)/shard_map/all_to_all | solution.py:178
  17.8 0.0 copy-done
  17.8 0.0 copy-done.5
  17.8 0.0 copy-done.4
  17.9 0.0 copy-start.1
  17.9 1.6 %copy-done.1 = bf16[1,1,64,128,128]{4,3,2,1,0:T(8,128)(2,1)S(1)} copy-done((bf16[1,1,64,128,128]{4,3,2,1,0:T(8,128)(2,1)S(1)}, bf16[1,1,64,128,128]{4,3,2,1,0:T(8,128)(2,1)}, u32[]{:S(2)}) %copy-start.1) | copy-done | bytes 2097176
  19.4 0.0 copy-start.2
  19.4 1.2 %copy-done.2 = bf16[2048,256]{1,0:T(8,128)(2,1)S(1)} copy-done((bf16[2048,256]{1,0:T(8,128)(2,1)S(1)}, bf16[2048,256]{1,0:T(8,128)(2,1)}, u32[]{:S(2)}) %copy-start.2) | copy-done | bytes 1048600
  20.7 0.0 copy-start.3
  20.7 0.0 copy-start.6
  20.7 7.2 %rating_tiles.1.grad_in = f32[12,128,256]{2,1,0:T(8,128)S(1)} custom-call(s32[64]{0:T(128)S(1)} %bitcast.24, s32[64]{0:T(128)S(1)} %bitcast.25, s32[1]{0:T(128)} %bitcast.15.cnt, bf16[16,128,256]{2,1,0:T(8,128)(2,1)S(1)} %bitcast.21, bf16[12,128,256]{2,1,0:T(8,128)(2,1)S(1)} %bitcast.18, bf16[64,128,128]{2,1,0:T(8,128)(2,1)S(1)} %bitcast.20), custom_call_target="tpu_custom_call" | custom-call | flops 1073741824 | bytes 5505024 | tf_op jit(solution)/shard_map/rating_tiles/pallas_call | solution.py:180
  27.9 0.0 all-to-all-done.incoming
  27.9 0.0 copy-done.3
  27.9 0.0 copy-done.6
  27.9 0.9 %graph_blocks.1 = f32[12,128,256]{2,1,0:T(8,128)S(1)} custom-call(s32[8]{0:T(128)S(1)} %bitcast.26, bf16[8,128,128]{2,1,0:T(8,128)(2,1)S(1)} %bitcast.22, bf16[8,128,256]{2,1,0:T(8,128)(2,1)S(1)} %all-to-all-done.incoming, f32[12,128,256]{2,1,0:T(8,128)S(1)} %rating_tiles.1.grad_in), custom_call_target="tpu_custom_call" | custom-call | tf_op jit(solution)/shard_map/graph_blocks/pallas_call | solution.py:196
  28.8 53.1 %reduce_update.1 = f32[16,256]{1,0:T(8,128)S(1)} custom-call(f32[8,12,16,256]{3,2,1,0:T(8,128)S(1)} %bitcast.16, bf16[96,16,256]{2,1,0:T(8,128)(2,1)S(1)} %bitcast.19), custom_call_target="tpu_custom_call" | custom-call | tf_op jit(solution)/shard_map/reduce_update/pallas_call | solution.py:205
  81.9 0.6 copy.12
  (1 shorter events, 0.0 us)
Async XLA Ops:
  0.0 17.8 %copy-start = (bf16[1,1536,256]{2,1,0:T(8,128)(2,1)S(1)}, bf16[1,1536,256]{2,1,0:T(8,128)(2,1)}, u32[]{:S(2)}) copy-start(bf16[1,1536,256]{2,1,0:T(8,128)(2,1)} %param.10) | copy-start | bytes 2359300
  0.0 17.8 %copy-start.5 = (s32[1,1,64]{2,1,0:T(1,128)S(1)}, s32[1,1,64]{2,1,0:T(1,128)}, u32[]{:S(2)}) copy-start(s32[1,1,64]{2,1,0:T(1,128)} %param.13) | copy-start | bytes 772
  0.0 17.8 %copy-start.4 = (s32[1,1,64]{2,1,0:T(1,128)S(1)}, s32[1,1,64]{2,1,0:T(1,128)}, u32[]{:S(2)}) copy-start(s32[1,1,64]{2,1,0:T(1,128)} %param.12) | copy-start | bytes 772
  3.3 24.7 %all-to-all-start = ((bf16[8,128,256]{2,1,0:T(8,128)(2,1)}), bf16[8,128,256]{2,1,0:T(8,128)(2,1)S(1)}, u32[]{:S(2)}, u32[]{:S(2)}) async-start(bf16[8,128,256]{2,1,0:T(8,128)(2,1)} %gather_fusion), calls=%async_computation | async-start | bytes 1048576 | tf_op jit(solution)/shard_map/all_to_all | solution.py:178
  17.9 1.6 %copy-start.1 = (bf16[1,1,64,128,128]{4,3,2,1,0:T(8,128)(2,1)S(1)}, bf16[1,1,64,128,128]{4,3,2,1,0:T(8,128)(2,1)}, u32[]{:S(2)}) copy-start(bf16[1,1,64,128,128]{4,3,2,1,0:T(8,128)(2,1)} %param.11) | copy-start | bytes 6291460
  19.4 1.2 %copy-start.2 = (bf16[2048,256]{1,0:T(8,128)(2,1)S(1)}, bf16[2048,256]{1,0:T(8,128)(2,1)}, u32[]{:S(2)}) copy-start(bf16[2048,256]{1,0:T(8,128)(2,1)} %param.9) | copy-start | bytes 3145732
  20.7 7.3 %copy-start.3 = (bf16[1,1,8,128,128]{4,3,2,1,0:T(8,128)(2,1)S(1)}, bf16[1,1,8,128,128]{4,3,2,1,0:T(8,128)(2,1)}, u32[]{:S(2)}) copy-start(bf16[1,1,8,128,128]{4,3,2,1,0:T(8,128)(2,1)} %param.17) | copy-start | bytes 786436
  20.7 7.3 %copy-start.6 = (s32[1,1,8]{2,1,0:T(1,128)S(1)}, s32[1,1,8]{2,1,0:T(1,128)}, u32[]{:S(2)}) copy-start(s32[1,1,8]{2,1,0:T(1,128)} %param.16) | copy-start | bytes 100

commit v2 on v0

v2 whole, which is shorter than its diff:
```python
import functools

import jax
import jax.numpy as jnp
from jax import lax
from jax.experimental import pallas as pl
from jax.experimental.pallas import tpu as pltpu
from jax.sharding import PartitionSpec as P

NZ = 12
CORES = 2
UNROLL = 8
MESH = pl.DeviceIdType.MESH
VMEM = pltpu.VMEM
F32 = jnp.float32
BF16 = jnp.bfloat16


def kernel(
    ny, nz, nx,
    tu, ti, cnt, sl, tg, users_hbm, items_hbm, ratings_hbm, sim_hbm, chunks_hbm,
    out,
    users, items, ratings, sim, mine, users_t, picked, incoming, parts, grad,
    send_a, send_b, recv_a, recv_b, acc_a, acc_b, recv2_a, recv2_b,
    squares, recv_p, recv_q,
    ssem, rsem, lsem,
):
    row = lax.axis_index("rows")
    col = lax.axis_index("cols")
    y = row // nz
    z = lax.rem(row, nz)
    x = col // CORES
    core = lax.rem(col, CORES)
    nc = nx * CORES
    slots, tile = ratings.shape[0], ratings.shape[1]
    rank = users.shape[-1]
    chunk = grad.shape[2]
    half = rank // 2
    ntiles = items.shape[0]
    zero = slots + nc

    def fetch(src, dst, which):
        copy = pltpu.make_async_copy(src, dst, lsem.at[which])
        copy.start()
        return copy

    group = slots // 4
    item_copy = fetch(items_hbm, items, 0)
    user_copy = fetch(users_hbm, users, 1)
    rating_copies = [
        fetch(ratings_hbm.at[pl.ds(g * group, group)], ratings.at[pl.ds(g * group, group)], 4 + g)
        for g in range(4)
    ]
    sim_copy = fetch(sim_hbm, sim, 2)
    mine_copy = fetch(chunks_hbm.at[row], mine, 3)

    def at(dy, dz, dx, dk):
        return {
            "rows": lax.rem(y + dy, ny) * nz + lax.rem(z + dz, nz),
            "cols": lax.rem(x + dx, nx) * CORES + lax.rem(core + dk, CORES),
        }

    along_z = [(lax.rem(z + d, nz), {"rows": y * nz + lax.rem(z + d, nz)}) for d in range(nz)]
    along_y = [(lax.rem(y + d, ny), {"rows": lax.rem(y + d, ny) * nz + z}) for d in range(ny)]
    along_c = [(lax.rem(col + d, nc), {"cols": lax.rem(col + d, nc)}) for d in range(nc)]
    first_ring = [at(0, n // CORES, 0, n % CORES) for n in range(1, nz * CORES)]
    second_ring = [at(n // nx, 0, n % nx, 0) for n in range(1, ny * nx)]

    barrier = pltpu.get_barrier_semaphore()
    partners = [o[1] for o in along_c[1:] + along_y[1:] + along_z[1:]]
    partners += [at(0, n // CORES, 0, n % CORES) for n in range(1, nz * CORES) if n % CORES and n // CORES]
    partners += [at(n // nx, 0, n % nx, 0) for n in range(1, ny * nx) if n % nx and n // nx]
    for device in partners:
        pl.semaphore_signal(barrier, inc=1, device_id=device, device_id_type=MESH)

    def push(src, dst, which, device):
        pltpu.make_async_remote_copy(
            src_ref=src, dst_ref=dst, send_sem=ssem.at[which], recv_sem=rsem.at[which],
            device_id=device, device_id_type=MESH,
        ).start()

    def whole(src, dst, which):
        return pltpu.make_async_remote_copy(
            src_ref=src, dst_ref=dst, send_sem=ssem.at[which], recv_sem=rsem.at[which],
            device_id=along_c[1][1], device_id_type=MESH,
        )

    item_copy.wait()
    for d in range(1, nc):
        picked[d - 1] = items[sl[along_c[d][0]]]
    pl.semaphore_wait(barrier, len(partners))
    for d in range(1, nc):
        push(picked.at[d - 1], incoming.at[d - 1], 0, along_c[d][1])

    parts[zero] = jnp.zeros((tile, rank), F32)
    user_copy.wait()
    for i in range(users.shape[0]):
        users_t[i] = users[i].T
    count = cnt[0]

    def link(last, item, place):
        before = jnp.int32(zero)
        for i in range(ntiles):
            hit = item == i
            before = jnp.where(hit, last[i], before)
            last[i] = jnp.where(hit, place, last[i])
        return before

    def tiles(g, carry):
        last = list(carry)
        found = []
        for u in range(UNROLL):
            t = g * UNROLL + u
            user, item = tu[t], ti[t]
            pred = jnp.dot(items[item], users_t[user], preferred_element_type=F32)
            diff = pred - ratings[t].T.astype(F32)
            err = jnp.where(t < count, diff, 0.0).astype(BF16)
            found.append((t, item, jnp.dot(err, users[user], preferred_element_type=F32)))
        for t, item, part in found:
            parts[t] = part + parts[link(last, item, t)]
        return tuple(last)

    last = tuple(jnp.int32(zero) for _ in range(ntiles))
    steps = group // UNROLL
    for g in range(4):
        rating_copies[g].wait()
        last = lax.fori_loop(g * steps, (g + 1) * steps, tiles, last)

    last = list(last)
    sim_copy.wait()
    for d in range(nc):
        source = lax.rem(col + nc - d, nc)
        if d == 0:
            panel = items[sl[source]]
        else:
            if d == 1:
                whole(picked, incoming, 0).wait_recv()
            panel = incoming[d - 1]
        part = jnp.dot(sim[source], panel, preferred_element_type=F32)
        parts[slots + d] = part + parts[link(last, tg[source], slots + d)]
    per_tile = tile // chunk
    for i in range(ntiles):
        value = parts[last[i]]
        for j in range(per_tile):
            n = i * per_tile + j
            grad[n // nz, n % nz] = value[j * chunk:(j + 1) * chunk]

    for d in range(1, max(ny, nz)):
        if d < nz:
            other, device = along_z[d]
            send_a[d - 1] = grad[:, other, :, :half].astype(BF16)
            push(send_a.at[d - 1], recv_a.at[d - 1], 1, device)
        if d < ny:
            other, device = along_y[d]
            send_b[d - 1] = grad[other, :, :, half:]
            push(send_b.at[d - 1], recv_b.at[d - 1], 2, device)

    whole(send_b, recv_b, 2).wait_recv()
    total = grad[y, :, :, half:]
    for d in range(ny - 1):
        total = total + recv_b[d]
    acc_b[...] = total
    for d in range(1, nz):
        push(acc_b.at[along_z[d][0]], recv2_b.at[d - 1], 3, along_z[d][1])

    whole(send_a, recv_a, 1).wait_recv()
    total = grad[:, z, :, :half]
    for d in range(nz - 1):
        total = total + recv_a[d].astype(F32)
    acc_a[...] = total
    for d in range(1, ny):
        push(acc_a.at[along_y[d][0]], recv2_a.at[d - 1], 4, along_y[d][1])

    whole(acc_b.at[pl.ds(0, nz - 1)], recv2_b, 3).wait_recv()
    own_b = acc_b[z]
    for d in range(nz - 1):
        own_b = own_b + recv2_b[d]
    whole(acc_a.at[pl.ds(0, ny - 1)], recv2_a, 4).wait_recv()
    own_a = acc_a[y]
    for d in range(ny - 1):
        own_a = own_a + recv2_a[d]

    part = jnp.sum(own_a * own_a + own_b * own_b, axis=0, keepdims=True)
    for n, (ring, recv) in enumerate(((first_ring, recv_p), (second_ring, recv_q))):
        squares[n] = part
        for d, device in enumerate(ring):
            push(squares.at[n], recv.at[d], 5 + n, device)
        whole(recv, recv, 5 + n).wait_recv()
        part = part + jnp.sum(recv[...], axis=0)
    entries = nc * ny * nz * chunk * rank
    root = jnp.sqrt(jnp.sum(part, axis=1, keepdims=True) / entries + 1e-06)

    mine_copy.wait()
    mixed = mine[...].astype(F32)
    out[:, :half] = mixed[:, :half] - 0.5 * own_a / root
    out[:, half:] = mixed[:, half:] - 0.5 * own_b / root

    whole(picked, incoming, 0).wait_send()
    whole(send_a, recv_a, 1).wait_send()
    whole(send_b, recv_b, 2).wait_send()
    whole(acc_b.at[pl.ds(0, nz - 1)], recv2_b, 3).wait_send()
    whole(acc_a.at[pl.ds(0, ny - 1)], recv2_a, 4).wait_send()
    whole(recv_p, recv_p, 5).wait_send()
    whole(recv_q, recv_q, 6).wait_send()


def shards(
    users, items, ratings, tile_users, tile_items, tile_count, send_list, block_target, similarity
):
    icount, rank = items.shape[1:]
    tile = ratings.shape[-1]
    slots = ratings.shape[2]
    ntiles = icount // tile
    utiles = users.shape[0] // tile
    nrows = lax.axis_size("rows")
    nc = lax.axis_size("cols")
    nz, ny, nx = NZ, nrows // NZ, nc // CORES
    chunk = icount // nrows
    half = rank // 2
    smem = pl.BlockSpec(memory_space=pltpu.SMEM)
    hbm = pl.BlockSpec(memory_space=pltpu.HBM)

    updated = pl.pallas_call(
        functools.partial(kernel, ny, nz, nx),
        out_shape=jax.ShapeDtypeStruct((chunk, rank), F32),
        in_specs=[smem] * 5 + [hbm] * 5,
        out_specs=pl.BlockSpec(memory_space=VMEM),
        scratch_shapes=[
            VMEM((utiles, tile, rank), BF16),
            VMEM((ntiles, tile, rank), BF16),
            VMEM((slots, tile, tile), BF16),
            VMEM((nc, tile, tile), BF16),
            VMEM((chunk, rank), BF16),
            VMEM((utiles, rank, tile), BF16),
            VMEM((nc - 1, tile, rank), BF16),
            VMEM((nc - 1, tile, rank), BF16),
            VMEM((slots + nc + 1, tile, rank), F32),
            VMEM((ny, nz, chunk, rank), F32),
            VMEM((nz - 1, ny, chunk, half), BF16),
            VMEM((ny - 1, nz, chunk, half), F32),
            VMEM((nz - 1, ny, chunk, half), BF16),
            VMEM((ny - 1, nz, chunk, half), F32),
            VMEM((ny, chunk, half), F32),
            VMEM((nz, chunk, half), F32),
            VMEM((ny - 1, chunk, half), F32),
            VMEM((nz - 1, chunk, half), F32),
            VMEM((2, 1, half), F32),
            VMEM((nz * CORES - 1, 1, half), F32),
            VMEM((ny * nx - 1, 1, half), F32),
            pltpu.SemaphoreType.DMA((7,)),
            pltpu.SemaphoreType.DMA((7,)),
            pltpu.SemaphoreType.DMA((8,)),
        ],
        compiler_params=pltpu.CompilerParams(
            collective_id=0, has_side_effects=True, vmem_limit_bytes=60 << 20
        ),
        name="item_update",
    )(
        tile_users[0, 0], tile_items[0, 0], tile_count[0],
        send_list[0, 0].reshape(-1), block_target[0, 0],
        users.reshape(-1, tile, rank), items[0].reshape(-1, tile, rank),
        ratings[0, 0], similarity[0, 0], items[0].reshape(nrows, chunk, rank),
    )
    return updated[None]


def solution(mesh):
    in_specs = (
        P("rows", None),
        P("cols", None, None),
        P("rows", "cols", None, None, None),
        P("rows", "cols", None),
        P("rows", "cols", None),
        P("rows", "cols"),
        P("rows", "cols", None, None),
        P("rows", "cols", None),
        P("rows", "cols", None, None, None),
    )
    out_specs = P("cols", "rows", None)
    return jax.shard_map(shards, mesh=mesh, in_specs=in_specs, out_specs=out_specs, check_vma=False)
```

time: 874 us -> 71.8 us (0.08)
  waiting for transfers between devices: 671 us -> 0 us
  blocking collectives: 109 us -> 0 us
  Pallas kernels: 0 us -> 69.6 us
  matrix products: 32 us -> 0 us
  local copies, waits for them, and re-layouts: 25.7 us -> 1.32 us
  starting transfers between devices: 13.9 us -> 0 us
  between operations: 14.1 us -> 0.66 us
    reduce_scatter x1 -> x0, waiting for transfers between devices: 664 us -> none  [shards(): owned = lax.psum_scatter(flat, 'rows', scatter_dimension=0, tiled=True)]
    psum x1 -> x0, blocking collectives: 109 us -> none  [shards(): squares = lax.psum(jnp.sum(owned * owned), ('rows', 'cols'))]
    pallas_call x0 -> x1, Pallas kernels: none -> 69.6 us  [shards(): pl.pallas_call(functools.partial(kernel, ny, nz, nx), out_shape=jax.Shape...]
    dot_general x10 -> x0, matrix products: 32 us -> none  [the longest x4 20.9 us: tile_block(): jnp.einsum('kt,tbr->kbr', onehot, part, precision=lax.Precision.HIGHEST)]
    gather x9 -> x0, local copies, waits for them, and re-layouts: 20.8 us -> none  [the longest x4 10.9 us: tile_block(): right = panels[item_idx]]
    all_to_all x1 -> x0, starting transfers between devices: 13.9 us -> none  [shards(): lax.all_to_all(outgoing, 'cols', split_axis=0, concat_axis=0, tiled=True)]
  transfers between devices with their start and end apart: 2 -> 0, of which waited for: 2 -> 0; matrix products, arithmetic and copies ran while one was open for 0% -> 0% of each run, Pallas kernels for 0% -> 0%
where the time goes in v2:
time: 71.8 us; the launch traced here: 71.6 us
  Pallas kernels  69.6 us (97%)
  local copies, waits for them, and re-layouts  1.32 us (2%)
    pallas_call x1, Pallas kernels, shards(): pl.pallas_call(functools.partial(kernel, ny, nz, nx), out_shape=jax.Shape...  69.6 us

profile of v2, /device:TPU:1, one launch (start us, length us, event | category | flops | bytes accessed | tf_op | source)
XLA Modules:
  0.0 71.6 jit_solution(12727482335571661041)
XLA Ops:
  0.7 69.6 %item_update.1 = f32[16,256]{1,0:T(8,128)} custom-call(s32[64]{0:T(128)} %bitcast.18, s32[64]{0:T(128)} %bitcast.19, s32[1]{0:T(128)} %bitcast.11.cnt, s32[8]{0:T(128)} %bitcast.20, s32[8]{0:T(128)} %bitcast.21, bf16[16,128,256]{2,1,0:T(8,128)(2,1)} %bitcast.15, bf16[12,128,256]{2,1,0:T(8,128)(2,1)} %bitcast.12, bf16[64,128,128]{2,1,0:T(8,128)(2,1)} %bitcast.14, ...), custom_call_target="tpu_custom_call" | custom-call | tf_op jit(solution)/shard_map/item_update/pallas_call | solution.py:223
  70.3 1.3 %copy.12 = f32[1,16,256]{2,1,0:T(8,128)} copy(f32[1,16,256]{2,1,0:T(8,128)} %bitcast.17) | data formatting | bytes 32768

commit v3 on v2

--- a/solution.py
+++ b/solution.py
@@ -14,15 +14,17 @@
 VMEM = pltpu.VMEM
 F32 = jnp.float32
 BF16 = jnp.bfloat16
+I16 = jnp.int16
+LEVELS = 32000.0
 
 
 def kernel(
     ny, nz, nx,
     tu, ti, cnt, sl, tg, users_hbm, items_hbm, ratings_hbm, sim_hbm, chunks_hbm,
     out,
-    users, items, ratings, sim, mine, users_t, picked, incoming, parts, grad,
-    send_a, send_b, recv_a, recv_b, acc_a, acc_b, recv2_a, recv2_b,
-    squares, recv_p, recv_q,
+    users, items, ratings, sim, mine, users_t, picked, incoming, parts, grad_a, grad_b,
+    send_a, send_b, recv_a, recv_b, acc_a, acc_b, send2_b, recv2_a, recv2_b,
+    squares, recv_p, recv_q, steps, step_a, step_b, step2_b,
     ssem, rsem, lsem,
 ):
     row = lax.axis_index("rows")
@@ -34,7 +36,7 @@
     nc = nx * CORES
     slots, tile = ratings.shape[0], ratings.shape[1]
     rank = users.shape[-1]
-    chunk = grad.shape[2]
+    chunk = grad_a.shape[2]
     half = rank // 2
     ntiles = items.shape[0]
     zero = slots + nc
@@ -63,13 +65,21 @@
     along_z = [(lax.rem(z + d, nz), {"rows": y * nz + lax.rem(z + d, nz)}) for d in range(nz)]
     along_y = [(lax.rem(y + d, ny), {"rows": lax.rem(y + d, ny) * nz + z}) for d in range(ny)]
     along_c = [(lax.rem(col + d, nc), {"cols": lax.rem(col + d, nc)}) for d in range(nc)]
-    first_ring = [at(0, n // CORES, 0, n % CORES) for n in range(1, nz * CORES)]
-    second_ring = [at(n // nx, 0, n % nx, 0) for n in range(1, ny * nx)]
+
+    def hops(d, size):
+        return min(d, size - d)
+
+    z_order = sorted(range(1, nz), key=lambda d: -hops(d, nz))
+    y_order = sorted(range(1, ny), key=lambda d: -hops(d, ny))
+    first = [(d, k) for d in range(nz) for k in range(CORES)][1:]
+    first.sort(key=lambda p: -hops(p[0], nz) - 0.3 * p[1])
+    second = [(d, e) for d in range(ny) for e in range(nx)][1:]
+    second.sort(key=lambda p: -hops(p[0], ny) - hops(p[1], nx))
+    first_ring = [at(0, d, 0, k) for d, k in first]
+    second_ring = [at(d, 0, e, 0) for d, e in second]
 
     barrier = pltpu.get_barrier_semaphore()
     partners = [o[1] for o in along_c[1:] + along_y[1:] + along_z[1:]]
-    partners += [at(0, n // CORES, 0, n % CORES) for n in range(1, nz * CORES) if n % CORES and n // CORES]
-    partners += [at(n // nx, 0, n % nx, 0) for n in range(1, ny * nx) if n % nx and n // nx]
     for device in partners:
         pl.semaphore_signal(barrier, inc=1, device_id=device, device_id_type=MESH)
 
@@ -87,10 +97,16 @@
 
     item_copy.wait()
     for d in range(1, nc):
-        picked[d - 1] = items[sl[along_c[d][0]]]
+        panel = items[sl[along_c[d][0]]]
+        picked[0, d - 1] = panel[:, :half]
+        picked[1, d - 1] = panel[:, half:]
     pl.semaphore_wait(barrier, len(partners))
-    for d in range(1, nc):
-        push(picked.at[d - 1], incoming.at[d - 1], 0, along_c[d][1])
+
+    def send_panels(h):
+        for d in range(1, nc):
+            push(picked.at[h, d - 1], incoming.at[h, d - 1], h, along_c[d][1])
+
+    send_panels(0)
 
     parts[zero] = jnp.zeros((tile, rank), F32)
     user_copy.wait()
@@ -121,61 +137,89 @@
         return tuple(last)
 
     last = tuple(jnp.int32(zero) for _ in range(ntiles))
-    steps = group // UNROLL
+    turns = group // UNROLL
     for g in range(4):
         rating_copies[g].wait()
-        last = lax.fori_loop(g * steps, (g + 1) * steps, tiles, last)
+        if g == 2:
+            whole(picked.at[0], incoming.at[0], 0).wait_send()
+            send_panels(1)
+        last = lax.fori_loop(g * turns, (g + 1) * turns, tiles, last)
 
     last = list(last)
+    sources = [lax.rem(col + nc - d, nc) for d in range(nc)]
+    before = [link(last, tg[sources[d]], slots + d) for d in range(nc)]
     sim_copy.wait()
-    for d in range(nc):
-        source = lax.rem(col + nc - d, nc)
-        if d == 0:
-            panel = items[sl[source]]
-        else:
-            if d == 1:
-                whole(picked, incoming, 0).wait_recv()
-            panel = incoming[d - 1]
-        part = jnp.dot(sim[source], panel, preferred_element_type=F32)
-        parts[slots + d] = part + parts[link(last, tg[source], slots + d)]
-    per_tile = tile // chunk
-    for i in range(ntiles):
-        value = parts[last[i]]
-        for j in range(per_tile):
-            n = i * per_tile + j
-            grad[n // nz, n % nz] = value[j * chunk:(j + 1) * chunk]
-
-    for d in range(1, max(ny, nz)):
-        if d < nz:
-            other, device = along_z[d]
-            send_a[d - 1] = grad[:, other, :, :half].astype(BF16)
-            push(send_a.at[d - 1], recv_a.at[d - 1], 1, device)
-        if d < ny:
-            other, device = along_y[d]
-            send_b[d - 1] = grad[other, :, :, half:]
-            push(send_b.at[d - 1], recv_b.at[d - 1], 2, device)
-
-    whole(send_b, recv_b, 2).wait_recv()
-    total = grad[y, :, :, half:]
+    parts[slots] = parts[before[0]] + jnp.dot(
+        sim[sources[0]], items[sl[col]], preferred_element_type=F32
+    )
+
+    def finish(h, grad):
+        cut = slice(h * half, (h + 1) * half)
+        whole(picked.at[h], incoming.at[h], h).wait_recv()
+        for d in range(1, nc):
+            part = jnp.dot(sim[sources[d]], incoming[h, d - 1], preferred_element_type=F32)
+            parts[slots + d, :, cut] = part + parts[before[d], :, cut]
+        top = jnp.zeros((8, half), F32)
+        for i in range(ntiles):
+            value = parts[last[i], :, cut]
+            top = jnp.maximum(top, jnp.max(jnp.abs(value).reshape(tile // 8, 8, half), axis=0))
+            for j in range(tile // chunk):
+                n = i * (tile // chunk) + j
+                grad[n // nz, n % nz] = value[j * chunk:(j + 1) * chunk]
+        return step_of(top)
+
+    def step_of(top):
+        top = jnp.max(jnp.max(top, axis=0, keepdims=True), axis=1, keepdims=True)
+        return jnp.maximum(top, 1e-20) / LEVELS
+
+    def code(value, inverse):
+        return jnp.round(value * inverse).astype(jnp.int32).astype(I16)
+
+    step = finish(0, grad_a)
+    steps[0] = jnp.broadcast_to(step, (1, half))
+    inverse = 1.0 / step
+    for d in z_order:
+        other, device = along_z[d]
+        push(steps.at[0], step_a.at[d - 1], 7, device)
+        send_a[d - 1] = code(grad_a[:, other], inverse)
+        push(send_a.at[d - 1], recv_a.at[d - 1], 2, device)
+    step = finish(1, grad_b)
+    steps[1] = jnp.broadcast_to(step, (1, half))
+    inverse = 1.0 / step
+    for d in y_order:
+        other, device = along_y[d]
+        push(steps.at[1], step_b.at[d - 1], 8, device)
+        send_b[d - 1] = code(grad_b[other], inverse)
+        push(send_b.at[d - 1], recv_b.at[d - 1], 3, device)
+
+    whole(step_b, step_b, 8).wait_recv()
+    whole(send_b, recv_b, 3).wait_recv()
+    total = grad_b[y]
     for d in range(ny - 1):
-        total = total + recv_b[d]
+        total = total + recv_b[d].astype(F32) * step_b[d]
     acc_b[...] = total
-    for d in range(1, nz):
-        push(acc_b.at[along_z[d][0]], recv2_b.at[d - 1], 3, along_z[d][1])
-
-    whole(send_a, recv_a, 1).wait_recv()
-    total = grad[:, z, :, :half]
+    step = step_of(jnp.max(jnp.abs(total).reshape(-1, 8, half), axis=0))
+    steps[2] = jnp.broadcast_to(step, (1, half))
+    send2_b[...] = code(total, 1.0 / step)
+    for d in z_order:
+        push(steps.at[2], step2_b.at[d - 1], 9, along_z[d][1])
+        push(send2_b.at[along_z[d][0]], recv2_b.at[d - 1], 4, along_z[d][1])
+
+    whole(step_a, step_a, 7).wait_recv()
+    whole(send_a, recv_a, 2).wait_recv()
+    total = grad_a[:, z]
     for d in range(nz - 1):
-        total = total + recv_a[d].astype(F32)
+        total = total + recv_a[d].astype(F32) * step_a[d]
     acc_a[...] = total
-    for d in range(1, ny):
-        push(acc_a.at[along_y[d][0]], recv2_a.at[d - 1], 4, along_y[d][1])
-
-    whole(acc_b.at[pl.ds(0, nz - 1)], recv2_b, 3).wait_recv()
+    for d in y_order:
+        push(acc_a.at[along_y[d][0]], recv2_a.at[d - 1], 10, along_y[d][1])
+
+    whole(step2_b, step2_b, 9).wait_recv()
+    whole(send2_b.at[pl.ds(0, nz - 1)], recv2_b, 4).wait_recv()
     own_b = acc_b[z]
     for d in range(nz - 1):
-        own_b = own_b + recv2_b[d]
-    whole(acc_a.at[pl.ds(0, ny - 1)], recv2_a, 4).wait_recv()
+        own_b = own_b + recv2_b[d].astype(F32) * step2_b[d]
+    whole(acc_a.at[pl.ds(0, ny - 1)], recv2_a, 10).wait_recv()
     own_a = acc_a[y]
     for d in range(ny - 1):
         own_a = own_a + recv2_a[d]
@@ -195,13 +239,16 @@
     out[:, :half] = mixed[:, :half] - 0.5 * own_a / root
     out[:, half:] = mixed[:, half:] - 0.5 * own_b / root
 
-    whole(picked, incoming, 0).wait_send()
-    whole(send_a, recv_a, 1).wait_send()
-    whole(send_b, recv_b, 2).wait_send()
-    whole(acc_b.at[pl.ds(0, nz - 1)], recv2_b, 3).wait_send()
-    whole(acc_a.at[pl.ds(0, ny - 1)], recv2_a, 4).wait_send()
+    whole(picked.at[1], incoming.at[1], 1).wait_send()
+    whole(send_a, recv_a, 2).wait_send()
+    whole(send_b, recv_b, 3).wait_send()
+    whole(send2_b.at[pl.ds(0, nz - 1)], recv2_b, 4).wait_send()
+    whole(acc_a.at[pl.ds(0, ny - 1)], recv2_a, 10).wait_send()
     whole(recv_p, recv_p, 5).wait_send()
     whole(recv_q, recv_q, 6).wait_send()
+    whole(step_a, step_a, 7).wait_send()
+    whole(step_b, step_b, 8).wait_send()
+    whole(step2_b, step2_b, 9).wait_send()
 
 
 def shards(
@@ -232,23 +279,29 @@
             VMEM((nc, tile, tile), BF16),
             VMEM((chunk, rank), BF16),
             VMEM((utiles, rank, tile), BF16),
-            VMEM((nc - 1, tile, rank), BF16),
-            VMEM((nc - 1, tile, rank), BF16),
+            VMEM((2, nc - 1, tile, half), BF16),
+            VMEM((2, nc - 1, tile, half), BF16),
             VMEM((slots + nc + 1, tile, rank), F32),
-            VMEM((ny, nz, chunk, rank), F32),
-            VMEM((nz - 1, ny, chunk, half), BF16),
-            VMEM((ny - 1, nz, chunk, half), F32),
-            VMEM((nz - 1, ny, chunk, half), BF16),
-            VMEM((ny - 1, nz, chunk, half), F32),
+            VMEM((ny, nz, chunk, half), F32),
+            VMEM((ny, nz, chunk, half), F32),
+            VMEM((nz - 1, ny, chunk, half), I16),
+            VMEM((ny - 1, nz, chunk, half), I16),
+            VMEM((nz - 1, ny, chunk, half), I16),
+            VMEM((ny - 1, nz, chunk, half), I16),
             VMEM((ny, chunk, half), F32),
             VMEM((nz, chunk, half), F32),
+            VMEM((nz, chunk, half), I16),
             VMEM((ny - 1, chunk, half), F32),
-            VMEM((nz - 1, chunk, half), F32),
+            VMEM((nz - 1, chunk, half), I16),
             VMEM((2, 1, half), F32),
             VMEM((nz * CORES - 1, 1, half), F32),
             VMEM((ny * nx - 1, 1, half), F32),
-            pltpu.SemaphoreType.DMA((7,)),
-            pltpu.SemaphoreType.DMA((7,)),
+            VMEM((3, 1, half), F32),
+            VMEM((nz - 1, 1, half), F32),
+            VMEM((ny - 1, 1, half), F32),
+            VMEM((nz - 1, 1, half), F32),
+            pltpu.SemaphoreType.DMA((11,)),
+            pltpu.SemaphoreType.DMA((11,)),
             pltpu.SemaphoreType.DMA((8,)),
         ],
         compiler_params=pltpu.CompilerParams(

time: 71.8 us -> 58.7 us (0.82)
  Pallas kernels: 69.6 us -> 56.5 us
    pallas_call x1, Pallas kernels: 69.6 us -> 56.5 us  [shards(): pl.pallas_call(functools.partial(kernel, ny, nz, nx), out_shape=jax.Shape...]
where the time goes in v3:
time: 58.7 us; the launch traced here: 58.5 us
  Pallas kernels  56.5 us (96%)
  local copies, waits for them, and re-layouts  1.32 us (2%)
  between operations  0.66 us (1%)
    pallas_call x1, Pallas kernels, shards(): pl.pallas_call(functools.partial(kernel, ny, nz, nx), out_shape=jax.Shape...  56.5 us
    unnamed x1, local copies, waits for them, and re-layouts  1.32 us

profile of v3, /device:TPU:1, one launch (start us, length us, event | category | flops | bytes accessed | tf_op | source)
XLA Modules:
  0.0 58.5 jit_solution(13168617894161390255)
XLA Ops:
  0.7 56.5 %item_update.1 = f32[16,256]{1,0:T(8,128)} custom-call(s32[64]{0:T(128)} %bitcast.18, s32[64]{0:T(128)} %bitcast.19, s32[1]{0:T(128)} %bitcast.11.cnt, s32[8]{0:T(128)} %bitcast.20, s32[8]{0:T(128)} %bitcast.21, bf16[16,128,256]{2,1,0:T(8,128)(2,1)} %bitcast.15, bf16[12,128,256]{2,1,0:T(8,128)(2,1)} %bitcast.12, bf16[64,128,128]{2,1,0:T(8,128)(2,1)} %bitcast.14, ...), custom_call_target="tpu_custom_call" | custom-call | tf_op jit(solution)/shard_map/item_update/pallas_call | solution.py:270
  57.1 1.3 %copy.12 = f32[1,16,256]{2,1,0:T(8,128)} copy(f32[1,16,256]{2,1,0:T(8,128)} %bitcast.17) | data formatting | bytes 32768

commit v4 on v3

--- a/solution.py
+++ b/solution.py
@@ -20,9 +20,9 @@
 
 def kernel(
     ny, nz, nx,
-    tu, ti, cnt, sl, tg, users_hbm, items_hbm, ratings_hbm, sim_hbm, chunks_hbm,
+    cnt, tu_hbm, ti_hbm, sl_hbm, tg_hbm, users_hbm, items_hbm, ratings_hbm, sim_hbm, chunks_hbm,
     out,
-    users, items, ratings, sim, mine, users_t, picked, incoming, parts, grad_a, grad_b,
+    tu, ti, sl, tg, users, items, ratings, sim, mine, users_t, picked, incoming, parts, grad_a, grad_b,
     send_a, send_b, recv_a, recv_b, acc_a, acc_b, send2_b, recv2_a, recv2_b,
     squares, recv_p, recv_q, steps, step_a, step_b, step2_b,
     ssem, rsem, lsem,
@@ -47,11 +47,16 @@
         return copy
 
     group = slots // 4
+    list_copy = fetch(sl_hbm, sl, 8)
     item_copy = fetch(items_hbm, items, 0)
     user_copy = fetch(users_hbm, users, 1)
     rating_copies = [
         fetch(ratings_hbm.at[pl.ds(g * group, group)], ratings.at[pl.ds(g * group, group)], 4 + g)
         for g in range(4)
+    ]
+    index_copies = [
+        fetch(src, dst, 9 + n)
+        for n, (src, dst) in enumerate(((tu_hbm, tu), (ti_hbm, ti), (tg_hbm, tg)))
     ]
     sim_copy = fetch(sim_hbm, sim, 2)
     mine_copy = fetch(chunks_hbm.at[row], mine, 3)
@@ -95,6 +100,7 @@
             device_id=along_c[1][1], device_id_type=MESH,
         )
 
+    list_copy.wait()
     item_copy.wait()
     for d in range(1, nc):
         panel = items[sl[along_c[d][0]]]
@@ -112,6 +118,8 @@
     user_copy.wait()
     for i in range(users.shape[0]):
         users_t[i] = users[i].T
+    for copy in index_copies:
+        copy.wait()
     count = cnt[0]
 
     def link(last, item, place):
@@ -264,15 +272,18 @@
     nz, ny, nx = NZ, nrows // NZ, nc // CORES
     chunk = icount // nrows
     half = rank // 2
-    smem = pl.BlockSpec(memory_space=pltpu.SMEM)
     hbm = pl.BlockSpec(memory_space=pltpu.HBM)
 
     updated = pl.pallas_call(
         functools.partial(kernel, ny, nz, nx),
         out_shape=jax.ShapeDtypeStruct((chunk, rank), F32),
-        in_specs=[smem] * 5 + [hbm] * 5,
+        in_specs=[pl.BlockSpec(memory_space=pltpu.SMEM)] + [hbm] * 9,
         out_specs=pl.BlockSpec(memory_space=VMEM),
         scratch_shapes=[
+            pltpu.SMEM((slots,), jnp.int32),
+            pltpu.SMEM((slots,), jnp.int32),
+            pltpu.SMEM((nc,), jnp.int32),
+            pltpu.SMEM((nc,), jnp.int32),
             VMEM((utiles, tile, rank), BF16),
             VMEM((ntiles, tile, rank), BF16),
             VMEM((slots, tile, tile), BF16),
@@ -302,17 +313,22 @@
             VMEM((nz - 1, 1, half), F32),
             pltpu.SemaphoreType.DMA((11,)),
             pltpu.SemaphoreType.DMA((11,)),
-            pltpu.SemaphoreType.DMA((8,)),
+            pltpu.SemaphoreType.DMA((12,)),
         ],
         compiler_params=pltpu.CompilerParams(
-            collective_id=0, has_side_effects=True, vmem_limit_bytes=60 << 20
+            collective_id=0, has_side_effects=True, vmem_limit_bytes=40 << 20
         ),
         name="item_update",
     )(
-        tile_users[0, 0], tile_items[0, 0], tile_count[0],
-        send_list[0, 0].reshape(-1), block_target[0, 0],
-        users.reshape(-1, tile, rank), items[0].reshape(-1, tile, rank),
-        ratings[0, 0], similarity[0, 0], items[0].reshape(nrows, chunk, rank),
+        tile_count[0],
+        *(
+            pltpu.with_memory_space_constraint(a, pltpu.HBM)
+            for a in (
+                tile_users[0, 0], tile_items[0, 0], send_list[0, 0].reshape(-1), block_target[0, 0],
+                users.reshape(-1, tile, rank), items[0].reshape(-1, tile, rank),
+                ratings[0, 0], similarity[0, 0], items[0].reshape(nrows, chunk, rank),
+            )
+        ),
     )
     return updated[None]
 

time: 58.7 us -> 56.6 us (0.964)
  Pallas kernels: 56.5 us -> 55.2 us
  local copies, waits for them, and re-layouts: 1.32 us -> 0.61 us
    pallas_call x1, Pallas kernels: 56.5 us -> 55.2 us  [shards(): pl.pallas_call(functools.partial(kernel, ny, nz, nx), out_shape=jax.Shape...]
    unnamed x1, local copies, waits for them, and re-layouts: 1.32 us -> 0.61 us
where the time goes in v4:
time: 56.6 us; the launch traced here: 56.5 us
  Pallas kernels  55.2 us (98%)
  between operations  0.66 us (1%)
  local copies, waits for them, and re-layouts  0.61 us (1%)
    pallas_call x1, Pallas kernels, shards(): pl.pallas_call(functools.partial(kernel, ny, nz, nx), out_shape=jax.Shape...  55.2 us

profile of v4, /device:TPU:1, one launch (start us, length us, event | category | flops | bytes accessed | tf_op | source)
XLA Modules:
  0.0 56.5 jit_solution(3057701174603424854)
XLA Ops:
  0.7 55.2 %item_update.1 = f32[16,256]{1,0:T(8,128)S(1)} custom-call(s32[1]{0:T(128)} %bitcast.11.cnt, s32[64]{0:T(128)} %bitcast.18, s32[64]{0:T(128)} %bitcast.19, s32[8]{0:T(128)} %bitcast.20, s32[8]{0:T(128)} %bitcast.21, bf16[16,128,256]{2,1,0:T(8,128)(2,1)} %bitcast.16, bf16[12,128,256]{2,1,0:T(8,128)(2,1)} %bitcast.13, bf16[64,128,128]{2,1,0:T(8,128)(2,1)} %bitcast.15, ...), custom_call_target="tpu_custom_call" | custom-call | tf_op jit(solution)/shard_map/item_update/pallas_call | solution.py:277
  55.9 0.6 %copy.12 = f32[1,16,256]{2,1,0:T(8,128)} copy(f32[1,16,256]{2,1,0:T(8,128)S(1)} %bitcast.12) | data formatting | bytes 32768

commit v5 on v4

--- a/solution.py
+++ b/solution.py
@@ -9,7 +9,7 @@
 
 NZ = 12
 CORES = 2
-UNROLL = 8
+UNROLL = 16
 MESH = pl.DeviceIdType.MESH
 VMEM = pltpu.VMEM
 F32 = jnp.float32
@@ -23,8 +23,8 @@
     cnt, tu_hbm, ti_hbm, sl_hbm, tg_hbm, users_hbm, items_hbm, ratings_hbm, sim_hbm, chunks_hbm,
     out,
     tu, ti, sl, tg, users, items, ratings, sim, mine, users_t, picked, incoming, parts, grad_a, grad_b,
-    send_a, send_b, recv_a, recv_b, acc_a, acc_b, send2_b, recv2_a, recv2_b,
-    squares, recv_p, recv_q, steps, step_a, step_b, step2_b,
+    send_a, send_b, recv_a, recv_b, acc_a, acc_b, send2_a, send2_b, recv2_a, recv2_b,
+    squares, recv_p, recv_q, steps, step_a, step_b, step2_a, step2_b,
     ssem, rsem, lsem,
 ):
     row = lax.axis_index("rows")
@@ -49,6 +49,35 @@
     group = slots // 4
     list_copy = fetch(sl_hbm, sl, 8)
     item_copy = fetch(items_hbm, items, 0)
+
+    def at(dy, dz, dx, dk):
+        return {
+            "rows": lax.rem(y + dy, ny) * nz + lax.rem(z + dz, nz),
+            "cols": lax.rem(x + dx, nx) * CORES + lax.rem(core + dk, CORES),
+        }
+
+    along_z = [(lax.rem(z + d, nz), {"rows": y * nz + lax.rem(z + d, nz)}) for d in range(nz)]
+    along_y = [(lax.rem(y + d, ny), {"rows": lax.rem(y + d, ny) * nz + z}) for d in range(ny)]
+    along_c = [(lax.rem(col + d, nc), {"cols": lax.rem(col + d, nc)}) for d in range(nc)]
+
+    def hops(d, size):
+        return min(d, size - d)
+
+    z_order = sorted(range(1, nz), key=lambda d: -hops(d, nz))
+    c_order = sorted(range(1, nc), key=lambda d: -hops(d, nc))
+    y_order = sorted(range(1, ny), key=lambda d: -hops(d, ny))
+    first = [(d, k) for d in range(nz) for k in range(CORES)][1:]
+    first.sort(key=lambda p: -hops(p[0], nz) - 0.3 * p[1])
+    second = [(d, e) for d in range(ny) for e in range(nx)][1:]
+    second.sort(key=lambda p: -hops(p[0], ny) - hops(p[1], nx))
+    first_ring = [at(0, d, 0, k) for d, k in first]
+    second_ring = [at(d, 0, e, 0) for d, e in second]
+
+    barrier = pltpu.get_barrier_semaphore()
+    partners = [o[1] for o in along_c[1:] + along_y[1:] + along_z[1:]]
+    for device in partners:
+        pl.semaphore_signal(barrier, inc=1, device_id=device, device_id_type=MESH)
+
     user_copy = fetch(users_hbm, users, 1)
     rating_copies = [
         fetch(ratings_hbm.at[pl.ds(g * group, group)], ratings.at[pl.ds(g * group, group)], 4 + g)
@@ -61,33 +90,6 @@
     sim_copy = fetch(sim_hbm, sim, 2)
     mine_copy = fetch(chunks_hbm.at[row], mine, 3)
 
-    def at(dy, dz, dx, dk):
-        return {
-            "rows": lax.rem(y + dy, ny) * nz + lax.rem(z + dz, nz),
-            "cols": lax.rem(x + dx, nx) * CORES + lax.rem(core + dk, CORES),
-        }
-
-    along_z = [(lax.rem(z + d, nz), {"rows": y * nz + lax.rem(z + d, nz)}) for d in range(nz)]
-    along_y = [(lax.rem(y + d, ny), {"rows": lax.rem(y + d, ny) * nz + z}) for d in range(ny)]
-    along_c = [(lax.rem(col + d, nc), {"cols": lax.rem(col + d, nc)}) for d in range(nc)]
-
-    def hops(d, size):
-        return min(d, size - d)
-
-    z_order = sorted(range(1, nz), key=lambda d: -hops(d, nz))
-    y_order = sorted(range(1, ny), key=lambda d: -hops(d, ny))
-    first = [(d, k) for d in range(nz) for k in range(CORES)][1:]
-    first.sort(key=lambda p: -hops(p[0], nz) - 0.3 * p[1])
-    second = [(d, e) for d in range(ny) for e in range(nx)][1:]
-    second.sort(key=lambda p: -hops(p[0], ny) - hops(p[1], nx))
-    first_ring = [at(0, d, 0, k) for d, k in first]
-    second_ring = [at(d, 0, e, 0) for d, e in second]
-
-    barrier = pltpu.get_barrier_semaphore()
-    partners = [o[1] for o in along_c[1:] + along_y[1:] + along_z[1:]]
-    for device in partners:
-        pl.semaphore_signal(barrier, inc=1, device_id=device, device_id_type=MESH)
-
     def push(src, dst, which, device):
         pltpu.make_async_remote_copy(
             src_ref=src, dst_ref=dst, send_sem=ssem.at[which], recv_sem=rsem.at[which],
@@ -109,7 +111,7 @@
     pl.semaphore_wait(barrier, len(partners))
 
     def send_panels(h):
-        for d in range(1, nc):
+        for d in c_order:
             push(picked.at[h, d - 1], incoming.at[h, d - 1], h, along_c[d][1])
 
     send_panels(0)
@@ -219,18 +221,23 @@
     for d in range(nz - 1):
         total = total + recv_a[d].astype(F32) * step_a[d]
     acc_a[...] = total
+    step = step_of(jnp.max(jnp.abs(total).reshape(-1, 8, half), axis=0))
+    steps[3] = jnp.broadcast_to(step, (1, half))
+    send2_a[...] = code(total, 1.0 / step)
     for d in y_order:
-        push(acc_a.at[along_y[d][0]], recv2_a.at[d - 1], 10, along_y[d][1])
+        push(steps.at[3], step2_a.at[d - 1], 11, along_y[d][1])
+        push(send2_a.at[along_y[d][0]], recv2_a.at[d - 1], 10, along_y[d][1])
 
     whole(step2_b, step2_b, 9).wait_recv()
     whole(send2_b.at[pl.ds(0, nz - 1)], recv2_b, 4).wait_recv()
     own_b = acc_b[z]
     for d in range(nz - 1):
         own_b = own_b + recv2_b[d].astype(F32) * step2_b[d]
-    whole(acc_a.at[pl.ds(0, ny - 1)], recv2_a, 10).wait_recv()
+    whole(step2_a, step2_a, 11).wait_recv()
+    whole(send2_a.at[pl.ds(0, ny - 1)], recv2_a, 10).wait_recv()
     own_a = acc_a[y]
     for d in range(ny - 1):
-        own_a = own_a + recv2_a[d]
+        own_a = own_a + recv2_a[d].astype(F32) * step2_a[d]
 
     part = jnp.sum(own_a * own_a + own_b * own_b, axis=0, keepdims=True)
     for n, (ring, recv) in enumerate(((first_ring, recv_p), (second_ring, recv_q))):
@@ -251,7 +258,8 @@
     whole(send_a, recv_a, 2).wait_send()
     whole(send_b, recv_b, 3).wait_send()
     whole(send2_b.at[pl.ds(0, nz - 1)], recv2_b, 4).wait_send()
-    whole(acc_a.at[pl.ds(0, ny - 1)], recv2_a, 10).wait_send()
+    whole(send2_a.at[pl.ds(0, ny - 1)], recv2_a, 10).wait_send()
+    whole(step2_a, step2_a, 11).wait_send()
     whole(recv_p, recv_p, 5).wait_send()
     whole(recv_q, recv_q, 6).wait_send()
     whole(step_a, step_a, 7).wait_send()
@@ -301,18 +309,20 @@
             VMEM((ny - 1, nz, chunk, half), I16),
             VMEM((ny, chunk, half), F32),
             VMEM((nz, chunk, half), F32),
+            VMEM((ny, chunk, half), I16),
             VMEM((nz, chunk, half), I16),
-            VMEM((ny - 1, chunk, half), F32),
+            VMEM((ny - 1, chunk, half), I16),
             VMEM((nz - 1, chunk, half), I16),
             VMEM((2, 1, half), F32),
             VMEM((nz * CORES - 1, 1, half), F32),
             VMEM((ny * nx - 1, 1, half), F32),
-            VMEM((3, 1, half), F32),
+            VMEM((4, 1, half), F32),
             VMEM((nz - 1, 1, half), F32),
             VMEM((ny - 1, 1, half), F32),
+            VMEM((ny - 1, 1, half), F32),
             VMEM((nz - 1, 1, half), F32),
-            pltpu.SemaphoreType.DMA((11,)),
-            pltpu.SemaphoreType.DMA((11,)),
+            pltpu.SemaphoreType.DMA((12,)),
+            pltpu.SemaphoreType.DMA((12,)),
             pltpu.SemaphoreType.DMA((12,)),
         ],
         compiler_params=pltpu.CompilerParams(

time: 56.6 us -> 56.6 us (level)
  no operation moved by 1% of the time
where the time goes in v5:
time: 56.6 us; the launch traced here: 56.4 us
  Pallas kernels  55.2 us (98%)
  between operations  0.66 us (1%)
  local copies, waits for them, and re-layouts  0.61 us (1%)
    pallas_call x1, Pallas kernels, shards(): pl.pallas_call(functools.partial(kernel, ny, nz, nx), out_shape=jax.Shape...  55.2 us

profile of v5, /device:TPU:1, one launch (start us, length us, event | category | flops | bytes accessed | tf_op | source)
XLA Modules:
  0.0 56.4 jit_solution(9829994729008721160)
XLA Ops:
  0.7 55.2 %item_update.1 = f32[16,256]{1,0:T(8,128)S(1)} custom-call(s32[1]{0:T(128)} %bitcast.11.cnt, s32[64]{0:T(128)} %bitcast.18, s32[64]{0:T(128)} %bitcast.19, s32[8]{0:T(128)} %bitcast.20, s32[8]{0:T(128)} %bitcast.21, bf16[16,128,256]{2,1,0:T(8,128)(2,1)} %bitcast.16, bf16[12,128,256]{2,1,0:T(8,128)(2,1)} %bitcast.13, bf16[64,128,128]{2,1,0:T(8,128)(2,1)} %bitcast.15, ...), custom_call_target="tpu_custom_call" | custom-call | tf_op jit(solution)/shard_map/item_update/pallas_call | solution.py:285
  55.8 0.6 %copy.12 = f32[1,16,256]{2,1,0:T(8,128)} copy(f32[1,16,256]{2,1,0:T(8,128)S(1)} %bitcast.12) | data formatting | bytes 32768
